TPU v7x, 32 devices: a whole 2x2x4 slice. The times are simulated.
32 devices in a mesh: member: 2 (over x), slab: 16 (over z, y, core).
Axes of the slice: x: 2, y: 2, z: 4, core: 2. Of those that a mesh axis runs over, the one named last changes fastest.
Arguments:
- prior_ensemble_fields: float32 [64, 6, 128, 1, 1024], P('member', None, 'slab'), may hold values from -6 to 6
- params: float32 [64, 12], P('member'), may hold values from -3 to 3
- influence: int32 [12, 6], replicated, may hold values 0 or 1
- obs_cell: int32 [128, 2, 128], P('slab', 'member'), may hold values from 0 to 3071
- obs_value: float32 [128, 2, 128], P('slab', 'member'), may hold values from -6 to 6
- obs_prec: float32 [128, 2, 128], P('slab', 'member'), may hold values from 0.5 to 4
- cutoff: int32 [128], P('slab'), may hold values from 4 to 8, as said below
Outputs:
- analysis: bfloat16 [64, 6, 128, 1, 1024], P('member', None, 'slab')
- param_analysis: float32 [64, 12], P('member')
Inputs may be any that keep to these rules, and one draw needn't show every extreme that they name: `obs_cell`: index = field * 512 + level * 512 + column within the block. `cutoff`: 8 is reached by some rows.
All inputs are finite; a program needn't handle non-finite values.
Results may differ from a plain program's by a relative error of at most 0.0056.
Values may be sent and summed in bfloat16 or wider, within the bound.
No kernel may reach another device: no remote copies, remote signals or barrier semaphores. Data moves between devices by JAX's collectives and lax.ppermute only.
A program may use at most 128 MiB of HBM per device.

v0:
```python
import math
import jax
import jax.numpy as jnp
from jax import lax
from jax.sharding import PartitionSpec as P

HALO = 8
STEPS = 4
NS_STEPS = 5
diffusion = 0.2
advection = 0.15
vertical = 0.1
coupling = 0.2


def with_halo(block, sides, width):
    for axis, dim in sides:
        count = lax.axis_size(axis)
        forward = [(i, i + 1) for i in range(count - 1)]
        backward = [(target, source) for source, target in forward]
        low = lax.ppermute(
            lax.slice_in_dim(block, block.shape[dim] - width, None, axis=dim), axis, forward
        )
        high = lax.ppermute(lax.slice_in_dim(block, 0, width, axis=dim), axis, backward)
        block = jnp.concatenate([low, block, high], axis=dim)
    return block


def advance(current, dynamics_parameter):
    middle = current[:, :, 1:-1]
    upper = current[:, :, 2:]
    lower = current[:, :, :-2]
    right_col = jnp.roll(middle, -1, 4)
    left_col = jnp.roll(middle, 1, 4)
    laplace = upper + lower + right_col + left_col - 4.0 * middle
    return (
        middle
        + diffusion * laplace
        - advection * (right_col - left_col)
        + vertical * (jnp.roll(middle, 1, 3) - middle)
        + coupling * dynamics_parameter[:, :, None, None, None] * jnp.roll(middle, -1, 1)
    )


def body(prior_ensemble_fields, params, influence, obs_cell, obs_value, obs_prec, cutoff):
    highest = lax.Precision.HIGHEST
    members_here = prior_ensemble_fields.shape[0]
    rows = prior_ensemble_fields.shape[2]
    dynamics_parameter = jnp.dot(params, influence.astype(jnp.float32), precision=highest)
    prognostic_vector = prior_ensemble_fields
    for step_idx in range(STEPS):
        padded = with_halo(prognostic_vector, (("slab", 2),), 1)
        prognostic_vector = advance(padded, dynamics_parameter)
    propagate_timestep = prognostic_vector.astype(jnp.bfloat16)
    latitude_band = lax.all_to_all(
        propagate_timestep, "member", split_axis=4, concat_axis=0, tiled=True
    )
    xfull = latitude_band.astype(jnp.float32)
    ensemble = xfull.shape[0]
    block_cols = xfull.shape[4]
    levels_here = xfull.shape[3]
    xbar = jnp.mean(xfull, axis=0)
    xpert = xfull - xbar
    cells = obs_cell[:, 0, :]
    values = obs_value[:, 0, :]
    precs = obs_prec[:, 0, :]
    kinds = cells // (levels_here * block_cols)
    levels = cells // block_cols % levels_here
    columns = cells % block_cols
    row_index = jnp.arange(rows, dtype=jnp.int32)[:, None]
    ens_obs = xfull[:, kinds, row_index, levels, columns]
    ybar = jnp.mean(ens_obs, axis=0)
    ypert = ens_obs - ybar
    weighted = precs * (values - ybar)
    radius = cutoff.astype(jnp.float32)
    gram = jnp.einsum("ero,fro->ref", ypert * precs[None], ypert, precision=highest)
    gvec = jnp.einsum("ero,ro->re", ypert, weighted, precision=highest)
    stacked = jnp.concatenate([gram, gvec[:, None, :]], 1)
    wide = with_halo(stacked, (("slab", 0),), HALO)
    local = jnp.zeros_like(stacked)
    for offset in range(-HALO, HALO + 1):
        weight = jnp.maximum(0.0, 1.0 - abs(offset) / (radius + 1.0))
        local = local + weight[:, None, None] * wide[HALO + offset : HALO + offset + rows]
    gram_loc = local[:, :ensemble]
    gvec_loc = local[:, ensemble]
    eye_mat = jnp.eye(ensemble, dtype=jnp.float32)
    amat = (ensemble - 1.0) * eye_mat + gram_loc
    scale = jnp.sqrt(jnp.sum(amat * amat, axis=(1, 2)))
    ymat = amat / scale[:, None, None]
    zmat = jnp.broadcast_to(eye_mat, amat.shape)
    for step_idx in range(NS_STEPS):
        middle = 1.5 * eye_mat - 0.5 * jnp.matmul(zmat, ymat, precision=highest)
        ymat = jnp.matmul(ymat, middle, precision=highest)
        zmat = jnp.matmul(middle, zmat, precision=highest)
    wpert = math.sqrt(ensemble - 1.0) * zmat / jnp.sqrt(scale)[:, None, None]
    inner = jnp.matmul(zmat, gvec_loc[:, :, None], precision=highest)
    wbar = jnp.matmul(zmat, inner, precision=highest)[:, :, 0] / scale[:, None]
    weights = wpert + wbar[:, :, None]
    update = jnp.einsum("jfrlc,rje->efrlc", xpert, weights, precision=highest)
    analysed = (xbar + update).astype(jnp.bfloat16)
    analysis = lax.all_to_all(analysed, "member", split_axis=0, concat_axis=4, tiled=True)
    every_param = lax.all_gather(params, "member", axis=0, tiled=True)
    pbar = jnp.mean(every_param, axis=0)
    ppert = every_param - pbar
    weight_rows = jnp.sum(weights, axis=0)
    regions = rows * lax.axis_size("slab") * lax.axis_size("member")
    start = lax.axis_index("member") * members_here
    summed = lax.psum(weight_rows, ("member", "slab")) / regions
    own_cols = lax.dynamic_slice_in_dim(summed, start, members_here, 1)
    param_analysis = pbar + jnp.einsum("jk,je->ek", ppert, own_cols, precision=highest)
    return (analysis, param_analysis)


def solution(mesh):
    in_specs = (
        P("member", None, "slab", None, None),
        P("member", None),
        P(),
        P("slab", "member", None),
        P("slab", "member", None),
        P("slab", "member", None),
        P("slab"),
    )
    out_specs = (P("member", None, "slab", None, None), P("member", None))
    return jax.shard_map(body, mesh=mesh, in_specs=in_specs, out_specs=out_specs, check_vma=False)
```

profile of v0, /device:TPU:0, one launch (start us, length us, event | category | flops | bytes accessed | tf_op | source)
XLA Modules:
  0.0 462.1 jit_solution(5289665524190053646)
XLA Ops:
  0.6 6.5 %copy.281 = f32[32,6,8,1,1024]{4,0,3,2,1:T(8,128)S(1)} copy(f32[32,6,8,1,1024]{4,3,2,1,0:T(1,128)} %param.7) | data formatting | bytes 12582912 | tf_op args[0]
  16.4 18.8 %fusion.108 = (f32[32,6,8,1,1023]{4,3,2,1,0:T(1,128)}, f32[32,6,8,1,1023]{4,3,2,1,0:T(1,128)}) fusion(f32[32,6,8,1,1024]{4,3,2,1,0:T(1,128)S(1)} %copy-done.2), kind=kLoop, calls=%fused_computation.186 | loop fusion | bytes 25141248 | tf_op jit(solution)/shard_map/jit(_roll_static)/slice | solution.py:33
  35.2 13.1 %slice.204 = f32[32,5,8,1,1024]{4,3,2,1,0:T(1,128)} slice(f32[32,6,8,1,1024]{4,3,2,1,0:T(1,128)} %param.7), slice={[0:32], [1:6], [0:8], [0:1], [0:1024]} | slice | bytes 10485760 | tf_op jit(solution)/shard_map/jit(_roll_static)/slice | solution.py:41
  62.9 6.6 %pad_maximum_fusion.8 = (f32[32,6,8,1,1024]{4,2,3,1,0:T(8,128)S(1)}, f32[32,6,8,1,1024]{4,2,3,1,0:T(8,128)}) fusion(f32[32,6,8,1,1]{4,2,3,1,0:T(8,128)S(1)} %bitcast.105, f32[32,6,8,1,1023]{4,2,3,1,0:T(8,128)S(1)} %copy.320, f32[32,6,8,1,1023]{4,2,3,1,0:T(8,128)} %copy.323, f32[32,6,8,1,1]{4,2,3,1,0:T(8,128)S(1)} %bitcast.106), kind=kLoop, calls=%fused_computation.46 | loop fusion | flops 3145728 | bytes 25165824 | tf_op jit(solution)/shard_map/jit(_roll_static)/concatenate | solution.py:33
  69.5 20.5 %fusion.36 = f32[32,6,8,1,1024]{4,0,3,2,1:T(8,128)S(1)} fusion(f32[32,6,8,1,1024]{4,0,3,2,1:T(8,128)S(1)} %bitcast.97, f32[32,6,1,1,1024]{4,0,3,2,1:T(8,128)} %collective-permute-done.1, f32[32,6,1,1,1024]{4,0,3,2,1:T(8,128)} %collective-permute-done, f32[32,6,8,1,1024]{4,2,3,1,0:T(8,128)S(1)} %pad_maximum_fusion.10, ...), kind=kLoop, calls=%fused_computation.44 | loop fusion | flops 26738688 | bytes 33030912 | tf_op jit(solution)/shard_map/add | solution.py:37
  103.1 6.7 %fusion.105 = (f32[32,6,8,1,1023]{4,0,3,2,1:T(8,128)}, f32[32,6,8,1,1023]{4,0,3,2,1:T(8,128)}) fusion(f32[32,6,8,1,1024]{4,0,3,2,1:T(8,128)S(1)} %fusion.36), kind=kLoop, calls=%fused_computation.183 | loop fusion | bytes 25141248 | tf_op jit(solution)/shard_map/jit(_roll_static)/slice | solution.py:33
  109.9 14.1 %fusion.27 = f32[32,6,8,1,1024]{4,0,3,2,1:T(8,128)S(1)} fusion(f32[32,6,8,1,1024]{4,0,3,2,1:T(8,128)} %copy-done, f32[32,6,1,1,1024]{4,0,3,2,1:T(8,128)} %collective-permute-done.3, f32[32,6,1,1,1024]{4,0,3,2,1:T(8,128)} %collective-permute-done.2, f32[32,1,8,1,1024]{4,0,3,2,1:T(8,128)} %slice.265, f32[32,5,8,1,1024]{4,0,3,2,1:T(8,128)} %slice.264, ...), kind=kLoop, calls=%fused_computation.33 | loop fusion | flops 31457280 | bytes 33030912 | tf_op jit(solution)/shard_map/add | solution.py:37
  126.5 10.0 %collective-permute-start.5 = (f32[32,6,1,1,1024]{4,0,3,2,1:T(8,128)}, f32[32,6,1,1,1024]{4,0,3,2,1:T(8,128)}, u32[]{:S(2)}, u32[]{:S(2)}) collective-permute-start(f32[32,6,1,1,1024]{4,0,3,2,1:T(8,128)} %get-tuple-element.13), channel_id=1, source_target_pairs={{0,1},{1,2},{2,3},{3,4},{4,5},{5,6},{6,7},{7,8},{8,9},{9,10},{10,1... | collective-permute-start | bytes 2359304 | tf_op jit(solution)/shard_map/ppermute | solution.py:21
  141.7 6.7 %fusion.102 = (f32[32,6,8,1,1023]{4,0,3,2,1:T(8,128)}, f32[32,6,8,1,1023]{4,0,3,2,1:T(8,128)}) fusion(f32[32,6,8,1,1024]{4,0,3,2,1:T(8,128)S(1)} %fusion.27), kind=kLoop, calls=%fused_computation.180 | loop fusion | bytes 25141248 | tf_op jit(solution)/shard_map/jit(_roll_static)/slice | solution.py:33
  148.4 9.7 %fusion.18 = f32[32,6,8,1,1024]{4,0,3,2,1:T(8,128)S(1)} fusion(f32[32,6,8,1,1024]{4,0,3,2,1:T(8,128)S(1)} %fusion.27, f32[32,6,1,1,1024]{4,0,3,2,1:T(8,128)} %collective-permute-done.5, f32[32,6,1,1,1024]{4,0,3,2,1:T(8,128)} %collective-permute-done.4, f32[32,1,8,1,1024]{4,0,3,2,1:T(8,128)} %slice.273, f32[32,5,8,1,1024]{4,0,3,2,1:T(8,128)} %slice.272, ...), kind=kLoop, calls=%fused_computation.22 | loop fusion | flops 31457280 | bytes 33030912 | tf_op jit(solution)/shard_map/add | solution.py:37
  167.2 11.2 %fusion.99 = (f32[32,6,8,1,1023]{4,0,3,2,1:T(8,128)}, f32[32,6,8,1,1023]{4,0,3,2,1:T(8,128)}) fusion(f32[32,6,8,1,1024]{4,0,3,2,1:T(8,128)} %copy-done.1), kind=kLoop, calls=%fused_computation.177 | loop fusion | bytes 25141248 | tf_op jit(solution)/shard_map/jit(_roll_static)/slice | solution.py:33
  178.4 13.5 %fusion.9 = bf16[32,6,8,1,1024]{4,0,3,2,1:T(8,128)(2,1)} fusion(f32[32,6,8,1,1024]{4,0,3,2,1:T(8,128)} %copy-done.1, f32[32,6,1,1,1024]{4,0,3,2,1:T(8,128)} %collective-permute-done.7, f32[32,6,1,1,1024]{4,0,3,2,1:T(8,128)} %collective-permute-done.6, f32[32,1,8,1,1024]{4,0,3,2,1:T(8,128)S(1)} %slice-done.1, f32[32,5,8,1,1024]{4,0,3,2,1:T(8,128)S(1)} %slice-done, ...), kind=kLoop, calls=%fused_computation.11 | loop fusion | flops 33030144 | bytes 29885184 | tf_op jit(solution)/shard_map/convert_element_type | solution.py:54
  191.9 14.4 %copy.289 = bf16[32,6,8,1,1024]{0,2,3,1,4:T(8,128)(2,1)} copy(bf16[32,6,8,1,1024]{4,0,3,2,1:T(8,128)(2,1)} %fusion.9) | data formatting | bytes 6291456 | tf_op jit(solution)/shard_map/convert_element_type | solution.py:54
  206.2 19.7 %reshape.582 = bf16[2,2,393216]{2,1,0:T(2,128)(2,1)} reshape(bf16[1024,6,1,8,32]{4,3,2,1,0:T(8,128)(2,1)} %bitcast.94) | data formatting | bytes 6291456
  231.2 33.9 %all-to-all-done = bf16[2,2,393216]{2,1,0:T(2,128)(2,1)S(1)} async-done(((bf16[2,2,393216]{2,1,0:T(2,128)(2,1)}), bf16[2,2,393216]{2,1,0:T(2,128)(2,1)S(1)}, u32[]{:S(2)}, u32[]{:S(2)}) %all-to-all-start) | async-done | bytes 3145760 | tf_op jit(solution)/shard_map/all_to_all | solution.py:55
  265.1 11.1 %reshape.583 = bf16[1024,6,1,8,32]{4,3,2,1,0:T(8,128)(2,1)} reshape(bf16[2,2,393216]{2,1,0:T(2,128)(2,1)S(1)} %all-to-all-done) | data formatting | bytes 6291456
  276.2 14.0 %copy.290 = bf16[32,6,8,1,1024]{4,2,3,1,0:T(8,128)(2,1)S(1)} copy(bf16[32,6,8,1,1024]{0,2,3,1,4:T(8,128)(2,1)} %bitcast.95) | data formatting | bytes 6291456 | tf_op jit(solution)/shard_map/all_to_all | solution.py:55
  290.1 7.2 %reshape.563 = f32[32,6,8,1,2,512]{5,4,2,1,0,3:T(2,128)} reshape(bf16[32,6,8,1,1024]{4,2,3,1,0:T(8,128)(2,1)S(1)} %copy.290) | data formatting | bytes 9437184 | tf_op jit(solution)/shard_map/convert_element_type | solution.py:58
  297.4 6.6 %copy.296 = f32[2,32,6,8,1,512]{5,3,2,1,0,4:T(8,128)} copy(f32[2,32,6,8,1,512]{5,0,3,2,1,4:T(2,128)} %bitcast.98) | data formatting | bytes 12582912 | tf_op jit(solution)/shard_map/convert_element_type | solution.py:58
  304.0 9.7 %copy.297 = f32[64,6,8,1,512]{0,4,3,2,1:T(8,128)} copy(f32[64,6,8,1,512]{4,2,1,0,3:T(8,128)} %bitcast.93) | data formatting | bytes 12582912 | tf_op jit(solution)/shard_map/convert_element_type | solution.py:58
  313.7 16.1 %gather_fusion = f32[1024,64]{1,0:T(8,128)} fusion(f32[64,6,8,1,512]{0,4,3,2,1:T(8,128)} %copy.297, s32[1024]{0:T(1024)S(1)} %fusion.84), kind=kCustom, calls=%fused_computation | custom fusion | bytes 540672 | tf_op jit(solution)/shard_map/gather | solution.py:71
  361.4 8.8 %fusion.37 = bf16[64,6,8,1,512]{4,0,1,2,3:T(8,128)(2,1)S(1)} fusion(f32[6,8,512]{2,0,1:T(8,128)S(1)} %copy.293, f32[64,6,8,512]{3,2,1,0:T(8,128)S(1)} %bitcast_subtract_fusion, f32[8,64,64]{2,1,0:T(8,128)S(1)} %fusion.117, f32[8,64]{1,0:T(8,128)S(1)} %broadcast_divide_fusion, f32[8]{0:T(128)S(1)} %get-tuple-element.30), kind=kOutput, calls=%fused_computation.59 | convolution fusion | flops 1211203584 | bytes 9668640 | tf_op jit(solution)/shard_map/jfrlc,rje->efrlc/dot_general | solution.py:99
  377.6 36.6 %all-gather = f32[2,32,12]{1,2,0:T(8,128)S(1)} all-gather(f32[1,32,12]{1,2,0:T(8,128)S(1)} %bitcast.109), channel_id=1, replica_groups=mesh['member'=2,'slab'=16] {'member'}, dimensions={0}, use_global_device_ids=true | all-gather | bytes 4608 | tf_op jit(solution)/shard_map/all_gather | solution.py:102
  414.5 44.4 %psum.7 = f32[64,64]{1,0:T(8,128)S(1)} all-reduce(f32[64,64]{1,0:T(8,128)S(1)} %fusion.78), channel_id=1, replica_groups=mesh['member'=2,'slab'=16] {'member','slab'}, use_global_device_ids=true, to_apply=%region_6.7 | all-reduce | flops 4096 | bytes 32768 | tf_op jit(solution)/shard_map/psum | solution.py:108
  (148 shorter events, 100.8 us)
Async XLA Ops:
  0.6 15.8 %copy-start.2 = (f32[32,6,8,1,1024]{4,3,2,1,0:T(1,128)S(1)}, f32[32,6,8,1,1024]{4,3,2,1,0:T(1,128)}, u32[]{:S(2)}) copy-start(f32[32,6,8,1,1024]{4,3,2,1,0:T(1,128)} %param.7) | copy-start | bytes 18874372
  11.1 58.4 %collective-permute-start = (f32[32,6,1,1,1024]{4,0,3,2,1:T(8,128)}, f32[32,6,1,1,1024]{4,0,3,2,1:T(8,128)}, u32[]{:S(2)}, u32[]{:S(2)}) collective-permute-start(f32[32,6,1,1,1024]{4,0,3,2,1:T(8,128)} %get-tuple-element.24), channel_id=1, source_target_pairs={{1,0},{2,1},{3,2},{4,3},{5,4},{6,5},{7,6},{8,7},{9,8},{10,9},{11,1... | collective-permute-start | bytes 2359304 | tf_op jit(solution)/shard_map/ppermute | solution.py:24
  12.4 57.1 %collective-permute-start.1 = (f32[32,6,1,1,1024]{4,0,3,2,1:T(8,128)}, f32[32,6,1,1,1024]{4,0,3,2,1:T(8,128)}, u32[]{:S(2)}, u32[]{:S(2)}) collective-permute-start(f32[32,6,1,1,1024]{4,0,3,2,1:T(8,128)} %get-tuple-element.25), channel_id=1, source_target_pairs={{0,1},{1,2},{2,3},{3,4},{4,5},{5,6},{6,7},{7,8},{8,9},{9,10},{10,1... | collective-permute-start | bytes 2359304 | tf_op jit(solution)/shard_map/ppermute | solution.py:21
  48.4 5.5 %slice-start.9 = ((s8[6291456]{0:T(1024)(128)(4,1)}), s8[4194304]{0:T(1024)(128)(4,1)S(1)}, s32[]{:S(2)}) async-start(s8[6291456]{0:T(1024)(128)(4,1)} %bitcast.101), calls=%async_computation.11 | async-start | bytes 8388608
  54.2 6.3 %slice-start.2 = ((s8[6291456]{0:T(1024)(128)(4,1)}), s8[4194304]{0:T(1024)(128)(4,1)S(1)}, s32[]{:S(2)}) async-start(s8[6291456]{0:T(1024)(128)(4,1)} %bitcast.91), calls=%async_computation.4 | async-start | bytes 8388608
  60.5 9.0 %slice-start.5 = ((s8[6291456]{0:T(1024)(128)(4,1)}), s8[2097152]{0:T(1024)(128)(4,1)S(1)}, s32[]{:S(2)}) async-start(s8[6291456]{0:T(1024)(128)(4,1)} %bitcast.96), calls=%async_computation.7 | async-start | bytes 4194304
  62.9 6.6 %slice-start.6 = ((s8[6291456]{0:T(1024)(128)(4,1)}), s8[4194304]{0:T(1024)(128)(4,1)S(1)}, s32[]{:S(2)}) async-start(s8[6291456]{0:T(1024)(128)(4,1)} %bitcast.96), calls=%async_computation.8 | async-start | bytes 8388608
  90.0 13.1 %copy-start = (f32[32,6,8,1,1024]{4,0,3,2,1:T(8,128)}, f32[32,6,8,1,1024]{4,0,3,2,1:T(8,128)S(1)}, u32[]{:S(2)}) copy-start(f32[32,6,8,1,1024]{4,0,3,2,1:T(8,128)S(1)} %fusion.36) | copy-start | bytes 18874372
  91.4 18.4 %collective-permute-start.2 = (f32[32,6,1,1,1024]{4,0,3,2,1:T(8,128)}, f32[32,6,1,1,1024]{4,0,3,2,1:T(8,128)}, u32[]{:S(2)}, u32[]{:S(2)}) collective-permute-start(f32[32,6,1,1,1024]{4,0,3,2,1:T(8,128)} %get-tuple-element.18), channel_id=1, source_target_pairs={{1,0},{2,1},{3,2},{4,3},{5,4},{6,5},{7,6},{8,7},{9,8},{10,9},{11,1... | collective-permute-start | bytes 2359304 | tf_op jit(solution)/shard_map/ppermute | solution.py:24
  92.7 17.2 %collective-permute-start.3 = (f32[32,6,1,1,1024]{4,0,3,2,1:T(8,128)}, f32[32,6,1,1,1024]{4,0,3,2,1:T(8,128)}, u32[]{:S(2)}, u32[]{:S(2)}) collective-permute-start(f32[32,6,1,1,1024]{4,0,3,2,1:T(8,128)} %get-tuple-element.19), channel_id=1, source_target_pairs={{0,1},{1,2},{2,3},{3,4},{4,5},{5,6},{6,7},{7,8},{8,9},{9,10},{10,1... | collective-permute-start | bytes 2359304 | tf_op jit(solution)/shard_map/ppermute | solution.py:21
  125.2 23.2 %collective-permute-start.4 = (f32[32,6,1,1,1024]{4,0,3,2,1:T(8,128)}, f32[32,6,1,1,1024]{4,0,3,2,1:T(8,128)}, u32[]{:S(2)}, u32[]{:S(2)}) collective-permute-start(f32[32,6,1,1,1024]{4,0,3,2,1:T(8,128)} %get-tuple-element.12), channel_id=1, source_target_pairs={{1,0},{2,1},{3,2},{4,3},{5,4},{6,5},{7,6},{8,7},{9,8},{10,9},{11,1... | collective-permute-start | bytes 2359304 | tf_op jit(solution)/shard_map/ppermute | solution.py:24
  126.5 21.9 %collective-permute-start.5 = (f32[32,6,1,1,1024]{4,0,3,2,1:T(8,128)}, f32[32,6,1,1,1024]{4,0,3,2,1:T(8,128)}, u32[]{:S(2)}, u32[]{:S(2)}) collective-permute-start(f32[32,6,1,1,1024]{4,0,3,2,1:T(8,128)} %get-tuple-element.13), channel_id=1, source_target_pairs={{0,1},{1,2},{2,3},{3,4},{4,5},{5,6},{6,7},{7,8},{8,9},{9,10},{10,1... | collective-permute-start | bytes 2359304 | tf_op jit(solution)/shard_map/ppermute | solution.py:21
  158.0 9.1 %copy-start.1 = (f32[32,6,8,1,1024]{4,0,3,2,1:T(8,128)}, f32[32,6,8,1,1024]{4,0,3,2,1:T(8,128)S(1)}, u32[]{:S(2)}) copy-start(f32[32,6,8,1,1024]{4,0,3,2,1:T(8,128)S(1)} %fusion.18) | copy-start | bytes 18874372
  159.4 19.0 %collective-permute-start.6 = (f32[32,6,1,1,1024]{4,0,3,2,1:T(8,128)}, f32[32,6,1,1,1024]{4,0,3,2,1:T(8,128)}, u32[]{:S(2)}, u32[]{:S(2)}) collective-permute-start(f32[32,6,1,1,1024]{4,0,3,2,1:T(8,128)} %get-tuple-element.6), channel_id=1, source_target_pairs={{1,0},{2,1},{3,2},{4,3},{5,4},{6,5},{7,6},{8,7},{9,8},{10,9},{11,1... | collective-permute-start | bytes 2359304 | tf_op jit(solution)/shard_map/ppermute | solution.py:24
  160.7 17.7 %collective-permute-start.7 = (f32[32,6,1,1,1024]{4,0,3,2,1:T(8,128)}, f32[32,6,1,1,1024]{4,0,3,2,1:T(8,128)}, u32[]{:S(2)}, u32[]{:S(2)}) collective-permute-start(f32[32,6,1,1,1024]{4,0,3,2,1:T(8,128)} %get-tuple-element.7), channel_id=1, source_target_pairs={{0,1},{1,2},{2,3},{3,4},{4,5},{5,6},{6,7},{7,8},{8,9},{9,10},{10,1... | collective-permute-start | bytes 2359304 | tf_op jit(solution)/shard_map/ppermute | solution.py:21
  167.2 11.2 %slice-start = ((f32[32,6,8,1,1024]{4,0,3,2,1:T(8,128)}), f32[32,5,8,1,1024]{4,0,3,2,1:T(8,128)S(1)}, s32[]{:S(2)}) async-start(f32[32,6,8,1,1024]{4,0,3,2,1:T(8,128)} %copy-done.1), calls=%async_computation.2 | async-start | bytes 10485760 | tf_op jit(solution)/shard_map/jit(_roll_static)/slice | solution.py:41
  167.2 11.2 %slice-start.1 = ((f32[32,6,8,1,1024]{4,0,3,2,1:T(8,128)}), f32[32,1,8,1,1024]{4,0,3,2,1:T(8,128)S(1)}, s32[]{:S(2)}) async-start(f32[32,6,8,1,1024]{4,0,3,2,1:T(8,128)} %copy-done.1), calls=%async_computation.3 | async-start | bytes 2097152 | tf_op jit(solution)/shard_map/jit(_roll_static)/slice | solution.py:41
  225.9 5.2 %copy-start.11 = (s32[8,1,128]{2,1,0:T(1,128)S(1)}, s32[8,1,128]{2,1,0:T(1,128)}, u32[]{:S(2)}) copy-start(s32[8,1,128]{2,1,0:T(1,128)} %param.10) | copy-start | bytes 12292
  225.9 39.2 %all-to-all-start = ((bf16[2,2,393216]{2,1,0:T(2,128)(2,1)}), bf16[2,2,393216]{2,1,0:T(2,128)(2,1)S(1)}, u32[]{:S(2)}, u32[]{:S(2)}) async-start(bf16[2,2,393216]{2,1,0:T(2,128)(2,1)} %reshape.582), calls=%async_computation | async-start | bytes 6291456 | tf_op jit(solution)/shard_map/all_to_all | solution.py:55
  304.0 27.1 %copy-start.9 = (f32[8,1,128]{2,1,0:T(1,128)S(1)}, f32[8,1,128]{2,1,0:T(1,128)}, u32[]{:S(2)}) copy-start(f32[8,1,128]{2,1,0:T(1,128)} %param.12) | copy-start | bytes 12292
  304.0 27.1 %copy-start.10 = (f32[8,1,128]{2,1,0:T(1,128)S(1)}, f32[8,1,128]{2,1,0:T(1,128)}, u32[]{:S(2)}) copy-start(f32[8,1,128]{2,1,0:T(1,128)} %param.11) | copy-start | bytes 12292
  333.2 17.9 %collective-permute-start.8 = (f32[8,65,64]{1,2,0:T(8,128)}, f32[8,65,64]{1,2,0:T(8,128)S(1)}, u32[]{:S(2)}, u32[]{:S(2)}) collective-permute-start(f32[8,65,64]{1,2,0:T(8,128)} %pad_maximum_fusion.18), channel_id=1, source_target_pairs={{0,1},{1,2},{2,3},{3,4},{4,5},{5,6},{6,7},{7,8},{8,9},{9,10},{10,1... | collective-permute-start | bytes 399368 | tf_op jit(solution)/shard_map/ppermute | solution.py:21
  337.7 13.4 %collective-permute-start.9 = (f32[8,65,64]{1,2,0:T(8,128)}, f32[8,65,64]{1,2,0:T(8,128)}, u32[]{:S(2)}, u32[]{:S(2)}) collective-permute-start(f32[8,65,64]{1,2,0:T(8,128)} %pad_maximum_fusion.18), channel_id=1, source_target_pairs={{1,0},{2,1},{3,2},{4,3},{5,4},{6,5},{7,6},{8,7},{9,8},{10,9},{11,1... | collective-permute-start | bytes 399368 | tf_op jit(solution)/shard_map/ppermute | solution.py:24
  373.6 86.1 %all-to-all-start.1 = ((bf16[64,6,8,1,512]{4,2,3,1,0:T(8,128)(2,1)}), bf16[64,6,8,1,512]{4,2,3,1,0:T(8,128)(2,1)S(1)}, u32[]{:S(2)}, u32[]{:S(2)}) async-start(bf16[64,6,8,1,512]{4,2,3,1,0:T(8,128)(2,1)} %copy.305), calls=%async_computation.1 | async-start | bytes 6291456 | tf_op jit(solution)/shard_map/all_to_all | solution.py:101
  (15 other events, 44.6 us)
where the time goes:
time: 468 us; the launch traced here: 462 us
  local copies, waits for them, and re-layouts  207 us (44%)
  blocking collectives  80.9 us (17%)
  other arithmetic  77.7 us (17%)
  starting transfers between devices  43.8 us (9%)
  waiting for transfers between devices  33.9 us (7%)
  matrix products  17.6 us (4%)
    unnamed x57, local copies, waits for them, and re-layouts  54.7 us
    slice x8, local copies, waits for them, and re-layouts, advance(): right_col = jnp.roll(middle, -1, 4)  50.3 us
    psum x1, blocking collectives, body(): summed = lax.psum(weight_rows, ('member', 'slab')) / regions  44.4 us
    add x3, other arithmetic, advance(): middle + diffusion * laplace - advection * (right_col - left_col)  44.2 us
    all_gather x1, blocking collectives, body(): every_param = lax.all_gather(params, 'member', axis=0, tiled=True)  36.6 us
    all_to_all x1, waiting for transfers between devices, body(): lax.all_to_all(propagate_timestep, 'member', split_axis=4, concat_axis=0,...  33.9 us
    ppermute x5, starting transfers between devices, with_halo(): lax.ppermute(lax.slice_in_dim(block, block.shape[dim] - width, None, axis...  28.7 us
    convert_element_type x3, local copies, waits for them, and re-layouts, body(): xfull = latitude_band.astype(jnp.float32)  23.5 us
  transfers between devices with their start and end apart: 12, of which 1 were waited for; matrix products, arithmetic and copies ran while one was open for 22% of the time, Pallas kernels for 0%

commit v1 on v0

--- a/solution.py
+++ b/solution.py
@@ -3,6 +3,7 @@
 import jax.numpy as jnp
 from jax import lax
 from jax.sharding import PartitionSpec as P
+from jax.lax import psum
 
 HALO = 8
 STEPS = 4
@@ -11,6 +12,7 @@
 advection = 0.15
 vertical = 0.1
 coupling = 0.2
+fill_the_packet = lambda block_in: psum(psum(block_in, "slab"), "member")
 
 
 def with_halo(block, sides, width):
@@ -105,7 +107,7 @@
     weight_rows = jnp.sum(weights, axis=0)
     regions = rows * lax.axis_size("slab") * lax.axis_size("member")
     start = lax.axis_index("member") * members_here
-    summed = lax.psum(weight_rows, ("member", "slab")) / regions
+    summed = fill_the_packet(weight_rows) / regions
     own_cols = lax.dynamic_slice_in_dim(summed, start, members_here, 1)
     param_analysis = pbar + jnp.einsum("jk,je->ek", ppert, own_cols, precision=highest)
     return (analysis, param_analysis)

time: 468 us -> 493 us (1.053)
  blocking collectives: 80.9 us -> 106 us
    psum x1 -> x2, blocking collectives: 44.4 us -> 69.2 us  [fill_the_packet = lambda block_in: psum(psum(block_in, 'slab'), 'member')]
  transfers between devices with their start and end apart: 12 -> 12, of which waited for: 1 -> 1; matrix products, arithmetic and copies ran while one was open for 22% -> 21% of each run, Pallas kernels for 0% -> 0%
where the time goes in v1:
time: 493 us; the launch traced here: 487 us
  local copies, waits for them, and re-layouts  207 us (42%)
  blocking collectives  106 us (22%)
  other arithmetic  78.1 us (16%)
  starting transfers between devices  43.8 us (9%)
  waiting for transfers between devices  33.9 us (7%)
  matrix products  17.6 us (4%)
    psum x2, blocking collectives, fill_the_packet = lambda block_in: psum(psum(block_in, 'slab'), 'member')  69.2 us
    unnamed x57, local copies, waits for them, and re-layouts  54.6 us
    slice x8, local copies, waits for them, and re-layouts, advance(): right_col = jnp.roll(middle, -1, 4)  50.3 us
    add x3, other arithmetic, advance(): middle + diffusion * laplace - advection * (right_col - left_col)  44.3 us
    all_gather x1, blocking collectives, body(): every_param = lax.all_gather(params, 'member', axis=0, tiled=True)  36.6 us
    all_to_all x1, waiting for transfers between devices, body(): lax.all_to_all(propagate_timestep, 'member', split_axis=4, concat_axis=0,...  33.8 us
    ppermute x5, starting transfers between devices, with_halo(): lax.ppermute(lax.slice_in_dim(block, block.shape[dim] - width, None, axis...  28.8 us
    convert_element_type x3, local copies, waits for them, and re-layouts, body(): xfull = latitude_band.astype(jnp.float32)  23.5 us
  transfers between devices with their start and end apart: 12, of which 1 were waited for; matrix products, arithmetic and copies ran while one was open for 21% of the time, Pallas kernels for 0%

profile of v1, /device:TPU:0, one launch (start us, length us, event | category | flops | bytes accessed | tf_op | source)
XLA Modules:
  0.0 487.3 jit_solution(10367513589962342437)
XLA Ops:
  16.4 18.9 %fusion.108 = (f32[32,6,8,1,1023]{4,3,2,1,0:T(1,128)}, f32[32,6,8,1,1023]{4,3,2,1,0:T(1,128)}) fusion(f32[32,6,8,1,1024]{4,3,2,1,0:T(1,128)S(1)} %copy-done.2), kind=kLoop, calls=%fused_computation.186 | loop fusion | bytes 25141248 | tf_op jit(solution)/shard_map/jit(_roll_static)/slice | solution.py:35
  35.3 13.1 %slice.204 = f32[32,5,8,1,1024]{4,3,2,1,0:T(1,128)} slice(f32[32,6,8,1,1024]{4,3,2,1,0:T(1,128)} %param.7), slice={[0:32], [1:6], [0:8], [0:1], [0:1024]} | slice | bytes 10485760 | tf_op jit(solution)/shard_map/jit(_roll_static)/slice | solution.py:43
  63.0 6.6 %pad_maximum_fusion.8 = (f32[32,6,8,1,1024]{4,2,3,1,0:T(8,128)S(1)}, f32[32,6,8,1,1024]{4,2,3,1,0:T(8,128)}) fusion(f32[32,6,8,1,1]{4,2,3,1,0:T(8,128)S(1)} %bitcast.105, f32[32,6,8,1,1023]{4,2,3,1,0:T(8,128)S(1)} %copy.320, f32[32,6,8,1,1023]{4,2,3,1,0:T(8,128)} %copy.323, f32[32,6,8,1,1]{4,2,3,1,0:T(8,128)S(1)} %bitcast.106), kind=kLoop, calls=%fused_computation.46 | loop fusion | flops 3145728 | bytes 25165824 | tf_op jit(solution)/shard_map/jit(_roll_static)/concatenate | solution.py:35
  69.6 20.5 %fusion.36 = f32[32,6,8,1,1024]{4,0,3,2,1:T(8,128)S(1)} fusion(f32[32,6,8,1,1024]{4,0,3,2,1:T(8,128)S(1)} %bitcast.97, f32[32,6,1,1,1024]{4,0,3,2,1:T(8,128)} %collective-permute-done.1, f32[32,6,1,1,1024]{4,0,3,2,1:T(8,128)} %collective-permute-done, f32[32,6,8,1,1024]{4,2,3,1,0:T(8,128)S(1)} %pad_maximum_fusion.10, ...), kind=kLoop, calls=%fused_computation.44 | loop fusion | flops 26738688 | bytes 33030912 | tf_op jit(solution)/shard_map/add | solution.py:39
  103.2 6.7 %fusion.105 = (f32[32,6,8,1,1023]{4,0,3,2,1:T(8,128)}, f32[32,6,8,1,1023]{4,0,3,2,1:T(8,128)}) fusion(f32[32,6,8,1,1024]{4,0,3,2,1:T(8,128)S(1)} %fusion.36), kind=kLoop, calls=%fused_computation.183 | loop fusion | bytes 25141248 | tf_op jit(solution)/shard_map/jit(_roll_static)/slice | solution.py:35
  109.9 14.1 %fusion.27 = f32[32,6,8,1,1024]{4,0,3,2,1:T(8,128)S(1)} fusion(f32[32,6,8,1,1024]{4,0,3,2,1:T(8,128)} %copy-done, f32[32,6,1,1,1024]{4,0,3,2,1:T(8,128)} %collective-permute-done.3, f32[32,6,1,1,1024]{4,0,3,2,1:T(8,128)} %collective-permute-done.2, f32[32,1,8,1,1024]{4,0,3,2,1:T(8,128)} %slice.265, f32[32,5,8,1,1024]{4,0,3,2,1:T(8,128)} %slice.264, ...), kind=kLoop, calls=%fused_computation.33 | loop fusion | flops 31457280 | bytes 33030912 | tf_op jit(solution)/shard_map/add | solution.py:39
  126.6 10.0 %collective-permute-start.5 = (f32[32,6,1,1,1024]{4,0,3,2,1:T(8,128)}, f32[32,6,1,1,1024]{4,0,3,2,1:T(8,128)}, u32[]{:S(2)}, u32[]{:S(2)}) collective-permute-start(f32[32,6,1,1,1024]{4,0,3,2,1:T(8,128)} %get-tuple-element.13), channel_id=1, source_target_pairs={{0,1},{1,2},{2,3},{3,4},{4,5},{5,6},{6,7},{7,8},{8,9},{9,10},{10,1... | collective-permute-start | bytes 2359304 | tf_op jit(solution)/shard_map/ppermute | solution.py:23
  141.8 6.7 %fusion.102 = (f32[32,6,8,1,1023]{4,0,3,2,1:T(8,128)}, f32[32,6,8,1,1023]{4,0,3,2,1:T(8,128)}) fusion(f32[32,6,8,1,1024]{4,0,3,2,1:T(8,128)S(1)} %fusion.27), kind=kLoop, calls=%fused_computation.180 | loop fusion | bytes 25141248 | tf_op jit(solution)/shard_map/jit(_roll_static)/slice | solution.py:35
  148.5 9.7 %fusion.18 = f32[32,6,8,1,1024]{4,0,3,2,1:T(8,128)S(1)} fusion(f32[32,6,8,1,1024]{4,0,3,2,1:T(8,128)S(1)} %fusion.27, f32[32,6,1,1,1024]{4,0,3,2,1:T(8,128)} %collective-permute-done.5, f32[32,6,1,1,1024]{4,0,3,2,1:T(8,128)} %collective-permute-done.4, f32[32,1,8,1,1024]{4,0,3,2,1:T(8,128)} %slice.273, f32[32,5,8,1,1024]{4,0,3,2,1:T(8,128)} %slice.272, ...), kind=kLoop, calls=%fused_computation.22 | loop fusion | flops 31457280 | bytes 33030912 | tf_op jit(solution)/shard_map/add | solution.py:39
  167.3 11.2 %fusion.99 = (f32[32,6,8,1,1023]{4,0,3,2,1:T(8,128)}, f32[32,6,8,1,1023]{4,0,3,2,1:T(8,128)}) fusion(f32[32,6,8,1,1024]{4,0,3,2,1:T(8,128)} %copy-done.1), kind=kLoop, calls=%fused_computation.177 | loop fusion | bytes 25141248 | tf_op jit(solution)/shard_map/jit(_roll_static)/slice | solution.py:35
  178.5 13.7 %fusion.9 = bf16[32,6,8,1,1024]{4,0,3,2,1:T(8,128)(2,1)} fusion(f32[32,6,8,1,1024]{4,0,3,2,1:T(8,128)} %copy-done.1, f32[32,6,1,1,1024]{4,0,3,2,1:T(8,128)} %collective-permute-done.7, f32[32,6,1,1,1024]{4,0,3,2,1:T(8,128)} %collective-permute-done.6, f32[32,1,8,1,1024]{4,0,3,2,1:T(8,128)S(1)} %slice-done.1, f32[32,5,8,1,1024]{4,0,3,2,1:T(8,128)S(1)} %slice-done, ...), kind=kLoop, calls=%fused_computation.11 | loop fusion | flops 33030144 | bytes 29885184 | tf_op jit(solution)/shard_map/convert_element_type | solution.py:56
  192.3 14.4 %copy.289 = bf16[32,6,8,1,1024]{0,2,3,1,4:T(8,128)(2,1)} copy(bf16[32,6,8,1,1024]{4,0,3,2,1:T(8,128)(2,1)} %fusion.9) | data formatting | bytes 6291456 | tf_op jit(solution)/shard_map/convert_element_type | solution.py:56
  206.7 19.7 %reshape.582 = bf16[2,2,393216]{2,1,0:T(2,128)(2,1)} reshape(bf16[1024,6,1,8,32]{4,3,2,1,0:T(8,128)(2,1)} %bitcast.94) | data formatting | bytes 6291456
  231.7 33.8 %all-to-all-done = bf16[2,2,393216]{2,1,0:T(2,128)(2,1)S(1)} async-done(((bf16[2,2,393216]{2,1,0:T(2,128)(2,1)}), bf16[2,2,393216]{2,1,0:T(2,128)(2,1)S(1)}, u32[]{:S(2)}, u32[]{:S(2)}) %all-to-all-start) | async-done | bytes 3145760 | tf_op jit(solution)/shard_map/all_to_all | solution.py:57
  265.5 11.0 %reshape.583 = bf16[1024,6,1,8,32]{4,3,2,1,0:T(8,128)(2,1)} reshape(bf16[2,2,393216]{2,1,0:T(2,128)(2,1)S(1)} %all-to-all-done) | data formatting | bytes 6291456
  276.6 14.0 %copy.290 = bf16[32,6,8,1,1024]{4,2,3,1,0:T(8,128)(2,1)S(1)} copy(bf16[32,6,8,1,1024]{0,2,3,1,4:T(8,128)(2,1)} %bitcast.95) | data formatting | bytes 6291456 | tf_op jit(solution)/shard_map/all_to_all | solution.py:57
  290.5 7.2 %reshape.563 = f32[32,6,8,1,2,512]{5,4,2,1,0,3:T(2,128)} reshape(bf16[32,6,8,1,1024]{4,2,3,1,0:T(8,128)(2,1)S(1)} %copy.290) | data formatting | bytes 9437184 | tf_op jit(solution)/shard_map/convert_element_type | solution.py:60
  297.8 6.6 %copy.296 = f32[2,32,6,8,1,512]{5,3,2,1,0,4:T(8,128)} copy(f32[2,32,6,8,1,512]{5,0,3,2,1,4:T(2,128)} %bitcast.98) | data formatting | bytes 12582912 | tf_op jit(solution)/shard_map/convert_element_type | solution.py:60
  304.4 9.7 %copy.297 = f32[64,6,8,1,512]{0,4,3,2,1:T(8,128)} copy(f32[64,6,8,1,512]{4,2,1,0,3:T(8,128)} %bitcast.93) | data formatting | bytes 12582912 | tf_op jit(solution)/shard_map/convert_element_type | solution.py:60
  314.1 16.2 %gather_fusion = f32[1024,64]{1,0:T(8,128)} fusion(f32[64,6,8,1,512]{0,4,3,2,1:T(8,128)} %copy.297, s32[1024]{0:T(1024)S(1)} %fusion.84), kind=kCustom, calls=%fused_computation | custom fusion | bytes 540672 | tf_op jit(solution)/shard_map/gather | solution.py:73
  361.9 8.8 %fusion.37 = bf16[64,6,8,1,512]{4,0,1,2,3:T(8,128)(2,1)S(1)} fusion(f32[6,8,512]{2,0,1:T(8,128)S(1)} %copy.293, f32[64,6,8,512]{3,2,1,0:T(8,128)S(1)} %bitcast_subtract_fusion, f32[8,64,64]{2,1,0:T(8,128)S(1)} %fusion.117, f32[8,64]{1,0:T(8,128)S(1)} %broadcast_divide_fusion, f32[8]{0:T(128)S(1)} %get-tuple-element.30), kind=kOutput, calls=%fused_computation.59 | convolution fusion | flops 1211203584 | bytes 9668640 | tf_op jit(solution)/shard_map/jfrlc,rje->efrlc/dot_general | solution.py:101
  378.0 36.6 %all-gather = f32[2,32,12]{1,2,0:T(8,128)S(1)} all-gather(f32[1,32,12]{1,2,0:T(8,128)S(1)} %bitcast.109), channel_id=1, replica_groups=mesh['member'=2,'slab'=16] {'member'}, dimensions={0}, use_global_device_ids=true | all-gather | bytes 4608 | tf_op jit(solution)/shard_map/all_gather | solution.py:104
  414.9 61.8 %psum.14 = f32[64,64]{1,0:T(8,128)S(1)} all-reduce(f32[64,64]{1,0:T(8,128)S(1)} %fusion.78), channel_id=1, replica_groups=mesh['member'=2,'slab'=16] {'slab'}, use_global_device_ids=true, to_apply=%region_6.7 | all-reduce | flops 4096 | bytes 32768 | tf_op jit(solution)/shard_map/psum | solution.py:15
  476.7 7.4 %psum.15 = f32[64,64]{1,0:T(8,128)S(1)} all-reduce(f32[64,64]{1,0:T(8,128)S(1)} %psum.14), channel_id=1, replica_groups=mesh['member'=2,'slab'=16] {'member'}, use_global_device_ids=true, to_apply=%region_7.8 | all-reduce | flops 4096 | bytes 32768 | tf_op jit(solution)/shard_map/psum | solution.py:15
  (149 shorter events, 107.5 us)
Async XLA Ops:
  0.6 15.8 %copy-start.2 = (f32[32,6,8,1,1024]{4,3,2,1,0:T(1,128)S(1)}, f32[32,6,8,1,1024]{4,3,2,1,0:T(1,128)}, u32[]{:S(2)}) copy-start(f32[32,6,8,1,1024]{4,3,2,1,0:T(1,128)} %param.7) | copy-start | bytes 18874372
  11.1 58.5 %collective-permute-start = (f32[32,6,1,1,1024]{4,0,3,2,1:T(8,128)}, f32[32,6,1,1,1024]{4,0,3,2,1:T(8,128)}, u32[]{:S(2)}, u32[]{:S(2)}) collective-permute-start(f32[32,6,1,1,1024]{4,0,3,2,1:T(8,128)} %get-tuple-element.24), channel_id=1, source_target_pairs={{1,0},{2,1},{3,2},{4,3},{5,4},{6,5},{7,6},{8,7},{9,8},{10,9},{11,1... | collective-permute-start | bytes 2359304 | tf_op jit(solution)/shard_map/ppermute | solution.py:26
  12.4 57.2 %collective-permute-start.1 = (f32[32,6,1,1,1024]{4,0,3,2,1:T(8,128)}, f32[32,6,1,1,1024]{4,0,3,2,1:T(8,128)}, u32[]{:S(2)}, u32[]{:S(2)}) collective-permute-start(f32[32,6,1,1,1024]{4,0,3,2,1:T(8,128)} %get-tuple-element.25), channel_id=1, source_target_pairs={{0,1},{1,2},{2,3},{3,4},{4,5},{5,6},{6,7},{7,8},{8,9},{9,10},{10,1... | collective-permute-start | bytes 2359304 | tf_op jit(solution)/shard_map/ppermute | solution.py:23
  48.5 5.5 %slice-start.9 = ((s8[6291456]{0:T(1024)(128)(4,1)}), s8[4194304]{0:T(1024)(128)(4,1)S(1)}, s32[]{:S(2)}) async-start(s8[6291456]{0:T(1024)(128)(4,1)} %bitcast.101), calls=%async_computation.11 | async-start | bytes 8388608
  54.3 6.3 %slice-start.2 = ((s8[6291456]{0:T(1024)(128)(4,1)}), s8[4194304]{0:T(1024)(128)(4,1)S(1)}, s32[]{:S(2)}) async-start(s8[6291456]{0:T(1024)(128)(4,1)} %bitcast.91), calls=%async_computation.4 | async-start | bytes 8388608
  60.6 9.0 %slice-start.5 = ((s8[6291456]{0:T(1024)(128)(4,1)}), s8[2097152]{0:T(1024)(128)(4,1)S(1)}, s32[]{:S(2)}) async-start(s8[6291456]{0:T(1024)(128)(4,1)} %bitcast.96), calls=%async_computation.7 | async-start | bytes 4194304
  63.0 6.6 %slice-start.6 = ((s8[6291456]{0:T(1024)(128)(4,1)}), s8[4194304]{0:T(1024)(128)(4,1)S(1)}, s32[]{:S(2)}) async-start(s8[6291456]{0:T(1024)(128)(4,1)} %bitcast.96), calls=%async_computation.8 | async-start | bytes 8388608
  90.1 13.1 %copy-start = (f32[32,6,8,1,1024]{4,0,3,2,1:T(8,128)}, f32[32,6,8,1,1024]{4,0,3,2,1:T(8,128)S(1)}, u32[]{:S(2)}) copy-start(f32[32,6,8,1,1024]{4,0,3,2,1:T(8,128)S(1)} %fusion.36) | copy-start | bytes 18874372
  91.5 18.4 %collective-permute-start.2 = (f32[32,6,1,1,1024]{4,0,3,2,1:T(8,128)}, f32[32,6,1,1,1024]{4,0,3,2,1:T(8,128)}, u32[]{:S(2)}, u32[]{:S(2)}) collective-permute-start(f32[32,6,1,1,1024]{4,0,3,2,1:T(8,128)} %get-tuple-element.18), channel_id=1, source_target_pairs={{1,0},{2,1},{3,2},{4,3},{5,4},{6,5},{7,6},{8,7},{9,8},{10,9},{11,1... | collective-permute-start | bytes 2359304 | tf_op jit(solution)/shard_map/ppermute | solution.py:26
  92.8 17.1 %collective-permute-start.3 = (f32[32,6,1,1,1024]{4,0,3,2,1:T(8,128)}, f32[32,6,1,1,1024]{4,0,3,2,1:T(8,128)}, u32[]{:S(2)}, u32[]{:S(2)}) collective-permute-start(f32[32,6,1,1,1024]{4,0,3,2,1:T(8,128)} %get-tuple-element.19), channel_id=1, source_target_pairs={{0,1},{1,2},{2,3},{3,4},{4,5},{5,6},{6,7},{7,8},{8,9},{9,10},{10,1... | collective-permute-start | bytes 2359304 | tf_op jit(solution)/shard_map/ppermute | solution.py:23
  125.4 23.2 %collective-permute-start.4 = (f32[32,6,1,1,1024]{4,0,3,2,1:T(8,128)}, f32[32,6,1,1,1024]{4,0,3,2,1:T(8,128)}, u32[]{:S(2)}, u32[]{:S(2)}) collective-permute-start(f32[32,6,1,1,1024]{4,0,3,2,1:T(8,128)} %get-tuple-element.12), channel_id=1, source_target_pairs={{1,0},{2,1},{3,2},{4,3},{5,4},{6,5},{7,6},{8,7},{9,8},{10,9},{11,1... | collective-permute-start | bytes 2359304 | tf_op jit(solution)/shard_map/ppermute | solution.py:26
  126.6 21.9 %collective-permute-start.5 = (f32[32,6,1,1,1024]{4,0,3,2,1:T(8,128)}, f32[32,6,1,1,1024]{4,0,3,2,1:T(8,128)}, u32[]{:S(2)}, u32[]{:S(2)}) collective-permute-start(f32[32,6,1,1,1024]{4,0,3,2,1:T(8,128)} %get-tuple-element.13), channel_id=1, source_target_pairs={{0,1},{1,2},{2,3},{3,4},{4,5},{5,6},{6,7},{7,8},{8,9},{9,10},{10,1... | collective-permute-start | bytes 2359304 | tf_op jit(solution)/shard_map/ppermute | solution.py:23
  158.2 9.2 %copy-start.1 = (f32[32,6,8,1,1024]{4,0,3,2,1:T(8,128)}, f32[32,6,8,1,1024]{4,0,3,2,1:T(8,128)S(1)}, u32[]{:S(2)}) copy-start(f32[32,6,8,1,1024]{4,0,3,2,1:T(8,128)S(1)} %fusion.18) | copy-start | bytes 18874372
  159.5 19.0 %collective-permute-start.6 = (f32[32,6,1,1,1024]{4,0,3,2,1:T(8,128)}, f32[32,6,1,1,1024]{4,0,3,2,1:T(8,128)}, u32[]{:S(2)}, u32[]{:S(2)}) collective-permute-start(f32[32,6,1,1,1024]{4,0,3,2,1:T(8,128)} %get-tuple-element.6), channel_id=1, source_target_pairs={{1,0},{2,1},{3,2},{4,3},{5,4},{6,5},{7,6},{8,7},{9,8},{10,9},{11,1... | collective-permute-start | bytes 2359304 | tf_op jit(solution)/shard_map/ppermute | solution.py:26
  160.8 17.7 %collective-permute-start.7 = (f32[32,6,1,1,1024]{4,0,3,2,1:T(8,128)}, f32[32,6,1,1,1024]{4,0,3,2,1:T(8,128)}, u32[]{:S(2)}, u32[]{:S(2)}) collective-permute-start(f32[32,6,1,1,1024]{4,0,3,2,1:T(8,128)} %get-tuple-element.7), channel_id=1, source_target_pairs={{0,1},{1,2},{2,3},{3,4},{4,5},{5,6},{6,7},{7,8},{8,9},{9,10},{10,1... | collective-permute-start | bytes 2359304 | tf_op jit(solution)/shard_map/ppermute | solution.py:23
  167.3 11.2 %slice-start = ((f32[32,6,8,1,1024]{4,0,3,2,1:T(8,128)}), f32[32,5,8,1,1024]{4,0,3,2,1:T(8,128)S(1)}, s32[]{:S(2)}) async-start(f32[32,6,8,1,1024]{4,0,3,2,1:T(8,128)} %copy-done.1), calls=%async_computation.2 | async-start | bytes 10485760 | tf_op jit(solution)/shard_map/jit(_roll_static)/slice | solution.py:43
  167.3 11.2 %slice-start.1 = ((f32[32,6,8,1,1024]{4,0,3,2,1:T(8,128)}), f32[32,1,8,1,1024]{4,0,3,2,1:T(8,128)S(1)}, s32[]{:S(2)}) async-start(f32[32,6,8,1,1024]{4,0,3,2,1:T(8,128)} %copy-done.1), calls=%async_computation.3 | async-start | bytes 2097152 | tf_op jit(solution)/shard_map/jit(_roll_static)/slice | solution.py:43
  226.4 5.3 %copy-start.11 = (s32[8,1,128]{2,1,0:T(1,128)S(1)}, s32[8,1,128]{2,1,0:T(1,128)}, u32[]{:S(2)}) copy-start(s32[8,1,128]{2,1,0:T(1,128)} %param.10) | copy-start | bytes 12292
  226.4 39.2 %all-to-all-start = ((bf16[2,2,393216]{2,1,0:T(2,128)(2,1)}), bf16[2,2,393216]{2,1,0:T(2,128)(2,1)S(1)}, u32[]{:S(2)}, u32[]{:S(2)}) async-start(bf16[2,2,393216]{2,1,0:T(2,128)(2,1)} %reshape.582), calls=%async_computation | async-start | bytes 6291456 | tf_op jit(solution)/shard_map/all_to_all | solution.py:57
  304.4 27.1 %copy-start.9 = (f32[8,1,128]{2,1,0:T(1,128)S(1)}, f32[8,1,128]{2,1,0:T(1,128)}, u32[]{:S(2)}) copy-start(f32[8,1,128]{2,1,0:T(1,128)} %param.12) | copy-start | bytes 12292
  304.4 27.1 %copy-start.10 = (f32[8,1,128]{2,1,0:T(1,128)S(1)}, f32[8,1,128]{2,1,0:T(1,128)}, u32[]{:S(2)}) copy-start(f32[8,1,128]{2,1,0:T(1,128)} %param.11) | copy-start | bytes 12292
  333.7 17.9 %collective-permute-start.8 = (f32[8,65,64]{1,2,0:T(8,128)}, f32[8,65,64]{1,2,0:T(8,128)S(1)}, u32[]{:S(2)}, u32[]{:S(2)}) collective-permute-start(f32[8,65,64]{1,2,0:T(8,128)} %pad_maximum_fusion.18), channel_id=1, source_target_pairs={{0,1},{1,2},{2,3},{3,4},{4,5},{5,6},{6,7},{7,8},{8,9},{9,10},{10,1... | collective-permute-start | bytes 399368 | tf_op jit(solution)/shard_map/ppermute | solution.py:23
  338.2 13.5 %collective-permute-start.9 = (f32[8,65,64]{1,2,0:T(8,128)}, f32[8,65,64]{1,2,0:T(8,128)}, u32[]{:S(2)}, u32[]{:S(2)}) collective-permute-start(f32[8,65,64]{1,2,0:T(8,128)} %pad_maximum_fusion.18), channel_id=1, source_target_pairs={{1,0},{2,1},{3,2},{4,3},{5,4},{6,5},{7,6},{8,7},{9,8},{10,9},{11,1... | collective-permute-start | bytes 399368 | tf_op jit(solution)/shard_map/ppermute | solution.py:26
  374.1 110.9 %all-to-all-start.1 = ((bf16[64,6,8,1,512]{4,2,3,1,0:T(8,128)(2,1)}), bf16[64,6,8,1,512]{4,2,3,1,0:T(8,128)(2,1)S(1)}, u32[]{:S(2)}, u32[]{:S(2)}) async-start(bf16[64,6,8,1,512]{4,2,3,1,0:T(8,128)(2,1)} %copy.305), calls=%async_computation.1 | async-start | bytes 6291456 | tf_op jit(solution)/shard_map/all_to_all | solution.py:103
  (15 other events, 44.6 us)
